TPU v7x, 128 devices: a whole 4x4x4 slice. The times are simulated.
128 devices in a mesh: row: 8 (over z, core), col: 16 (over y, x).
Axes of the slice: x: 4, y: 4, z: 4, core: 2. Of those that a mesh axis runs over, the one named last changes fastest.
Arguments:
- tokens: bfloat16 [512, 8192], P('row', 'col'), may hold values from -6 to 6
- weights: bfloat16 [2, 8192, 28672], P(None, 'col', 'row'), may hold values from -2 to 2
- adapter_in: bfloat16 [2, 64, 8192], P(None, None, 'col'), may hold values from -0.75 to 0.75
- adapter_out: bfloat16 [2, 64, 28672], P(None, None, 'row'), may hold values from -0.3 to 0.3
- magnitude: float32 [2, 28672], P(None, 'row'), may hold values from 0.5 to 2
- hidden_cot: bfloat16 [512, 28672], P('col', 'row'), may hold values from -0.29882812 to 0.29882812
Outputs:
- hidden: bfloat16 [512, 28672], P('col', 'row')
- grad_in: float32 [2, 64, 8192], P(None, None, 'col')
- grad_out: float32 [2, 64, 28672], P(None, None, 'row')
- grad_mag: float32 [2, 28672], P(None, 'row')
All inputs are finite; a program needn't handle non-finite values.
Results may differ from a plain program's by a relative error of at most 0.028.
Values may be sent and summed in bfloat16 or wider, within the bound.
A program may use at most 192 MiB of HBM per device.

v0:
```python
import jax
import jax.numpy as jnp
from jax import lax
from jax.sharding import PartitionSpec as P

EPSILON = 1e-06


def copy_for_each(value, axis):
    copies = jnp.broadcast_to(value, (lax.axis_size(axis), *value.shape))
    return lax.all_to_all(copies, axis, split_axis=0, concat_axis=0, tiled=True)


def over_copies(value, axis):
    everything = copy_for_each(value, axis)
    return jnp.sum(everything, axis=0)


def laid_out(pieces, dim):
    lengths = list(pieces.shape[1:])
    lengths[dim] *= pieces.shape[0]
    return jnp.moveaxis(pieces, 0, dim).reshape(lengths)


def gathered_copies(value, axis, dim):
    return laid_out(copy_for_each(value, axis), dim)


def of_everyone(value, axis):
    return copy_for_each(value, axis).astype(jnp.float32).sum(axis=0)


def cotangents(gate, up_proj, cot_rows):
    sigmoid_g = jax.nn.sigmoid(gate)
    cot_float = cot_rows.astype(jnp.float32)
    d_gate = (cot_float * up_proj * sigmoid_g * (1.0 + gate * (1.0 - sigmoid_g))).astype(
        jnp.bfloat16
    )
    d_up = (cot_float * gate * sigmoid_g).astype(jnp.bfloat16)
    return (d_gate, d_up)


def on_device(tokens, weights, adapter_in, adapter_out, magnitude, hidden_cot):
    in_float = adapter_in.astype(jnp.float32)
    out_float = adapter_out.astype(jnp.float32)
    low_rank = jnp.einsum(
        "prd,prf->pdf", adapter_in, adapter_out, preferred_element_type=jnp.float32
    )
    direction = weights.astype(jnp.float32) + low_rank
    square_sum = over_copies(jnp.sum(direction * direction, axis=1), "col")
    column_norm = jnp.sqrt(square_sum + EPSILON)
    merged = (direction * (magnitude / column_norm)[:, None, :]).astype(jnp.bfloat16)
    token_all = gathered_copies(tokens, "row", 0)
    share_rows = token_all.shape[0] // lax.axis_size("col")
    partial_value = jnp.einsum("td,pdf->ptf", token_all, merged, preferred_element_type=jnp.float32)
    summed = lax.psum(partial_value.astype(jnp.bfloat16), "col").astype(jnp.float32)
    gate, up_proj = (summed[0], summed[1])
    hidden_all = (gate * jax.nn.sigmoid(gate) * up_proj).astype(jnp.bfloat16)
    hidden = lax.dynamic_slice_in_dim(hidden_all, lax.axis_index("col") * share_rows, share_rows, 0)
    cot_all = lax.all_gather(hidden_cot, "col", axis=0, tiled=True)
    d_gate, d_up = cotangents(gate, up_proj, cot_all)
    d_stack = jnp.stack((d_gate, d_up), axis=0)
    grad_weight = jnp.einsum("td,ptf->pdf", token_all, d_stack, preferred_element_type=jnp.float32)
    coef_grad = magnitude / column_norm
    statistic = over_copies(jnp.sum(grad_weight * direction, axis=1), "col")
    coef_dir = magnitude * statistic / column_norm**3
    d_direction = coef_grad[:, None, :] * grad_weight - coef_dir[:, None, :] * direction
    right_part = jnp.einsum("prd,pdf->prf", in_float, d_direction, precision=lax.Precision.HIGHEST)
    grad_out = lax.psum(right_part.astype(jnp.bfloat16), "col").astype(jnp.float32)
    left_part = jnp.einsum("prf,pdf->prd", out_float, d_direction, precision=lax.Precision.HIGHEST)
    grad_in = of_everyone(left_part.astype(jnp.bfloat16), "row").astype(jnp.float32)
    grad_mag = statistic / column_norm
    return (hidden, grad_in, grad_out, grad_mag)


def solution(mesh):
    in_specs = (
        P("row", "col"),
        P(None, "col", "row"),
        P(None, None, "col"),
        P(None, None, "row"),
        P(None, "row"),
        P("col", "row"),
    )
    out_specs = (P("col", "row"), P(None, None, "col"), P(None, None, "row"), P(None, "row"))
    return jax.shard_map(
        on_device, mesh=mesh, in_specs=in_specs, out_specs=out_specs, check_vma=False
    )
```

profile of v0, /device:TPU:0, one launch (start us, length us, event | category | flops | bytes accessed | tf_op | source)
XLA Modules:
  0.0 371.1 jit_solution(17381849521522753354)
XLA Ops:
  8.4 8.6 %multiply_reduce_fusion = (f32[2,3584]{1,0:T(2,128)S(1)}, f32[2,512,3584]{2,1,0:T(8,128)}) fusion(bf16[2,64,512]{2,1,0:T(8,128)(2,1)} %param.8, bf16[2,64,3584]{2,1,0:T(8,128)(2,1)S(1)} %copy-done, bf16[2,512,3584]{2,1,0:T(8,128)(2,1)} %param.7), kind=kOutput, calls=%fused_computation.5 | convolution fusion | flops 484434944 | bytes 23097344 | tf_op jit(solution)/shard_map/prd,prf->pdf/dot_general | solution.py:46
  17.1 19.8 %all_to_all.20 = f32[16,2,3584]{2,1,0:T(2,128)S(1)} all-to-all(f32[16,2,3584]{2,1,0:T(2,128)S(1)} %broadcast_in_dim.15), channel_id=1, replica_groups=mesh['row'=8,'col'=16] {'col'}, dimensions={0} | all-to-all | bytes 917504 | tf_op jit(solution)/shard_map/all_to_all | solution.py:11
  37.8 5.2 %all-to-all-start.1 = ((bf16[8,64,512]{2,1,0:T(8,128)(2,1)}), bf16[8,64,512]{2,1,0:T(8,128)(2,1)S(1)}, u32[]{:S(2)}, u32[]{:S(2)}) async-start(bf16[8,64,512]{2,1,0:T(8,128)(2,1)} %broadcast_in_dim.16), calls=%async_computation.1 | async-start | bytes 1048576 | tf_op jit(solution)/shard_map/all_to_all | solution.py:11
  43.3 10.1 %all-to-all-done.1 = bf16[8,64,512]{2,1,0:T(8,128)(2,1)S(1)} async-done(((bf16[8,64,512]{2,1,0:T(8,128)(2,1)}), bf16[8,64,512]{2,1,0:T(8,128)(2,1)S(1)}, u32[]{:S(2)}, u32[]{:S(2)}) %all-to-all-start.1) | async-done | bytes 524320 | tf_op jit(solution)/shard_map/all_to_all | solution.py:11
  53.3 11.6 %fusion.12 = bf16[2,512,3584]{1,2,0:T(8,128)(2,1)} fusion(bf16[512,512,1]{1,0,2:T(8,128)(2,1)S(1)} %bitcast.53, f32[2,512,3584]{2,1,0:T(8,128)} %get-tuple-element.28, f32[2,3584]{1,0:T(2,128)S(1)} %fusion.30), kind=kOutput, calls=%fused_computation.23 | convolution fusion | flops 3769106432 | bytes 22573056 | tf_op jit(solution)/shard_map/td,pdf->ptf/dot_general | solution.py:55
  65.6 5.9 %copy.27 = bf16[512,3584]{0,1:T(8,128)(2,1)} copy(bf16[512,3584]{1,0:T(8,128)(2,1)} %all-gather.2.cloned.1.call-done) | data formatting | bytes 7340032 | tf_op jit(solution)/shard_map/all_gather | solution.py:60
  71.5 128.1 %all-reduce.3.cloned.1.call-done = bf16[2,512,3584]{1,2,0:T(8,128)(2,1)} async-done(((bf16[2,512,3584]{1,2,0:T(8,128)(2,1)}), bf16[2,512,3584]{1,2,0:T(8,128)(2,1)}) %all-reduce.3.cloned.1.call-update) | async-done | bytes 7340048 | tf_op jit(solution)/shard_map/psum | solution.py:56
  199.7 10.3 %convert_element_type.51 = f32[2,512,3584]{1,2,0:T(8,128)} convert(bf16[2,512,3584]{1,2,0:T(8,128)(2,1)} %all-reduce.3.cloned.1.call-done) | non-fusion elementwise | flops 3670016 | bytes 22020096 | tf_op jit(solution)/shard_map/convert_element_type | solution.py:56
  210.0 9.8 %fusion.20 = (bf16[1,512,3584]{1,2,0:T(8,128)(2,1)S(1)}, bf16[1,512,3584]{1,2,0:T(8,128)(2,1)S(1)}, f32[512,3584]{0,1:T(8,128)}) fusion(bf16[512,3584]{0,1:T(8,128)(2,1)} %copy.27, f32[2,512,3584]{1,2,0:T(8,128)} %convert_element_type.51), kind=kLoop, calls=%fused_computation.28 | loop fusion | flops 25690112 | bytes 33030144 | tf_op jit(solution)/shard_map/stack | solution.py:62
  219.8 10.6 %fusion.1 = (f32[2,3584]{1,0:T(2,128)S(1)}, f32[2,3584,512]{1,2,0:T(8,128)}) fusion(f32[2,512,3584]{2,1,0:T(8,128)} %get-tuple-element.28, bf16[512,512,1]{1,0,2:T(8,128)(2,1)S(1)} %bitcast.54, bf16[1,512,3584]{1,2,0:T(8,128)(2,1)S(1)} %get-tuple-element.21, bf16[1,512,3584]{1,2,0:T(8,128)(2,1)S(1)} %get-tuple-element.20), kind=kOutput, calls=%fused_computation.3 | convolution fusion | flops 3769099264 | bytes 37253120 | tf_op jit(solution)/shard_map/td,ptf->pdf/dot_general | solution.py:63
  230.4 0.9 broadcast_in_dim.17
  231.3 5.4 %all-to-all-start.2 = ((f32[16,2,3584]{2,1,0:T(2,128)}), f32[16,2,3584]{2,1,0:T(2,128)S(1)}, u32[]{:S(2)}, u32[]{:S(2)}) async-start(f32[16,2,3584]{2,1,0:T(2,128)} %broadcast_in_dim.17), calls=%async_computation.2 | async-start | bytes 917504 | tf_op jit(solution)/shard_map/all_to_all | solution.py:11
  236.9 10.4 %all-to-all-done.2 = f32[16,2,3584]{2,1,0:T(2,128)S(1)} async-done(((f32[16,2,3584]{2,1,0:T(2,128)}), f32[16,2,3584]{2,1,0:T(2,128)S(1)}, u32[]{:S(2)}, u32[]{:S(2)}) %all-to-all-start.2) | async-done | bytes 458784 | tf_op jit(solution)/shard_map/all_to_all | solution.py:11
  248.1 1.4 fusion.29
  249.5 14.3 %fusion.25 = bf16[2,64,512]{2,1,0:T(8,128)(2,1)S(1)} fusion(bf16[2,64,3584]{2,1,0:T(8,128)(2,1)S(1)} %copy-done, f32[2,3584,512]{1,2,0:T(8,128)} %get-tuple-element.30, f32[2,512,3584]{2,1,0:T(8,128)} %get-tuple-element.28, f32[2,3584]{1,0:T(2,128)S(1)} %get-tuple-element.26, f32[2,3584]{1,0:T(2,128)S(1)} %fusion.30), kind=kOutput, calls=%fused_computation.34 | convolution fusion | flops 2829647872 | bytes 30466048 | tf_op jit(solution)/shard_map/prf,pdf->prd/dot_general | solution.py:70
  263.9 13.3 %fusion.16 = bf16[2,64,3584]{2,1,0:T(8,128)(2,1)} fusion(bf16[2,64,512]{2,1,0:T(8,128)(2,1)S(1)} %copy-done.1, f32[2,3584,512]{1,2,0:T(8,128)} %get-tuple-element.30, f32[2,512,3584]{2,1,0:T(8,128)S(1)} %bitcast.52, f32[2,3584]{1,0:T(2,128)S(1)} %get-tuple-element.26, f32[2,3584]{1,0:T(2,128)S(1)} %fusion.30), kind=kOutput, calls=%fused_computation.26 | convolution fusion | flops 2830041088 | bytes 30466048 | tf_op jit(solution)/shard_map/prd,pdf->prf/dot_general | solution.py:68
  277.2 1.2 broadcast_in_dim.18
  278.4 4.4 %all-to-all-start.3 = ((bf16[8,2,64,512]{3,2,1,0:T(8,128)(2,1)}), bf16[8,2,64,512]{3,2,1,0:T(8,128)(2,1)S(1)}, u32[]{:S(2)}, u32[]{:S(2)}) async-start(bf16[8,2,64,512]{3,2,1,0:T(8,128)(2,1)} %broadcast_in_dim.18), calls=%async_computation.3 | async-start | bytes 2097152 | tf_op jit(solution)/shard_map/all_to_all | solution.py:11
  282.8 12.3 %slice_bitcast_fusion.1 = (f32[512,3584]{0,1:T(8,128)}, f32[512,3584]{0,1:T(8,128)}) fusion(f32[2,512,3584]{1,2,0:T(8,128)} %convert_element_type.51), kind=kLoop, calls=%fused_computation.16 | loop fusion | bytes 29360128 | tf_op jit(solution)/shard_map/squeeze | solution.py:57
  295.1 4.2 %fusion.21 = bf16[32,3584]{0,1:T(8,128)(2,1)S(1)} fusion(f32[512,3584]{0,1:T(8,128)} %get-tuple-element.24, s32[]{:T(128)S(6)} %select_n.3, f32[512,3584]{0,1:T(8,128)} %get-tuple-element.22, f32[512,3584]{0,1:T(8,128)} %get-tuple-element.23), kind=kLoop, calls=%fused_computation.31 | loop fusion | flops 344064 | bytes 1605636 | tf_op jit(solution)/shard_map/convert_element_type | solution.py:58
  299.2 1.0 copy.31
  300.2 60.9 %all-reduce.5.cloned.1.call-done = bf16[2,64,3584]{2,1,0:T(8,128)(2,1)} async-done(((bf16[2,64,3584]{2,1,0:T(8,128)(2,1)}), bf16[2,64,3584]{2,1,0:T(8,128)(2,1)}) %all-reduce.5.cloned.1.call-update) | async-done | bytes 917520 | tf_op jit(solution)/shard_map/psum | solution.py:69
  361.1 2.6 convert_element_type.61
  363.7 0.8 convert_reduce_fusion
  (30 shorter events, 4.1 us)
Async XLA Ops:
  7.2 1.2 copy-start
  7.2 58.4 %all-gather.2.cloned.1.call-start = ((), (), s32[]{:S(2)}) async-start(), calls=%async_computation.5 | async-start | bytes 3899392 | tf_op jit(solution)/shard_map/all_gather | solution.py:60
  8.4 28.6 %copy-start.3 = (bf16[64,512]{1,0:T(8,128)(2,1)S(1)}, bf16[64,512]{1,0:T(8,128)(2,1)}, u32[]{:S(2)}) copy-start(bf16[64,512]{1,0:T(8,128)(2,1)} %param.6) | copy-start | bytes 196612
  8.4 34.8 %copy-start.2 = (f32[2,3584]{1,0:T(2,128)S(1)}, f32[2,3584]{1,0:T(2,128)}, u32[]{:S(2)}) copy-start(f32[2,3584]{1,0:T(2,128)} %param.10) | copy-start | bytes 86020
  37.8 15.5 %all-to-all-start.1 = ((bf16[8,64,512]{2,1,0:T(8,128)(2,1)}), bf16[8,64,512]{2,1,0:T(8,128)(2,1)S(1)}, u32[]{:S(2)}, u32[]{:S(2)}) async-start(bf16[8,64,512]{2,1,0:T(8,128)(2,1)} %broadcast_in_dim.16), calls=%async_computation.1 | async-start | bytes 1048576 | tf_op jit(solution)/shard_map/all_to_all | solution.py:11
  43.0 156.7 %all-reduce.3.cloned.1.call-start = ((), (), s32[]{:S(2)}) async-start(), calls=%async_computation.4 | async-start | bytes 14680064 | tf_op jit(solution)/shard_map/psum | solution.py:56
  230.4 33.4 %slice-start = ((s8[14680064]{0:T(1024)(128)(4,1)}), s8[2097152]{0:T(1024)(128)(4,1)S(1)}, s32[]{:S(2)}) async-start(s8[14680064]{0:T(1024)(128)(4,1)} %bitcast.51), calls=%async_computation.7 | async-start | bytes 4194304
  231.3 16.0 %all-to-all-start.2 = ((f32[16,2,3584]{2,1,0:T(2,128)}), f32[16,2,3584]{2,1,0:T(2,128)S(1)}, u32[]{:S(2)}, u32[]{:S(2)}) async-start(f32[16,2,3584]{2,1,0:T(2,128)} %broadcast_in_dim.17), calls=%async_computation.2 | async-start | bytes 917504 | tf_op jit(solution)/shard_map/all_to_all | solution.py:11
  236.7 124.4 %all-reduce.5.cloned.1.call-start = ((), (), s32[]{:S(2)}) async-start(), calls=%async_computation.6 | async-start | bytes 1835008 | tf_op jit(solution)/shard_map/psum | solution.py:69
  249.5 14.4 %slice-start.1 = ((s8[14680064]{0:T(1024)(128)(4,1)}), s8[4194304]{0:T(1024)(128)(4,1)S(1)}, s32[]{:S(2)}) async-start(s8[14680064]{0:T(1024)(128)(4,1)} %bitcast.51), calls=%async_computation.8 | async-start | bytes 8388608
  249.5 14.4 %slice-start.2 = ((s8[14680064]{0:T(1024)(128)(4,1)}), s8[4194304]{0:T(1024)(128)(4,1)S(1)}, s32[]{:S(2)}) async-start(s8[14680064]{0:T(1024)(128)(4,1)} %bitcast.51), calls=%async_computation.9 | async-start | bytes 8388608
  249.5 14.4 %slice-start.3 = ((s8[14680064]{0:T(1024)(128)(4,1)}), s8[4194304]{0:T(1024)(128)(4,1)S(1)}, s32[]{:S(2)}) async-start(s8[14680064]{0:T(1024)(128)(4,1)} %bitcast.51), calls=%async_computation.10 | async-start | bytes 8388608
  249.5 14.4 %copy-start.1 = (bf16[2,64,512]{2,1,0:T(8,128)(2,1)S(1)}, bf16[2,64,512]{2,1,0:T(8,128)(2,1)}, u32[]{:S(2)}) copy-start(bf16[2,64,512]{2,1,0:T(8,128)(2,1)} %param.8) | copy-start | bytes 393220
  278.4 85.3 %all-to-all-start.3 = ((bf16[8,2,64,512]{3,2,1,0:T(8,128)(2,1)}), bf16[8,2,64,512]{3,2,1,0:T(8,128)(2,1)S(1)}, u32[]{:S(2)}, u32[]{:S(2)}) async-start(bf16[8,2,64,512]{3,2,1,0:T(8,128)(2,1)} %broadcast_in_dim.18), calls=%async_computation.3 | async-start | bytes 2097152 | tf_op jit(solution)/shard_map/all_to_all | solution.py:11
Sparse Core Ops, SparseCore 0:
  10.1 55.4 all-gather.1
  69.1 130.5 all-reduce.2
  277.4 83.7 all-reduce.4
where the time goes:
time: 372 us; the launch traced here: 371 us
  waiting for transfers between devices  211 us (57%)
  matrix products  58.4 us (16%)
  other arithmetic  30.1 us (8%)
  local copies, waits for them, and re-layouts  22.6 us (6%)
  blocking collectives  19.8 us (5%)
  starting transfers between devices  15.3 us (4%)
  between operations  13.9 us (4%)
    psum x1, waiting for transfers between devices, on_device(): lax.psum(partial_value.astype(jnp.bfloat16), 'col').astype(jnp.float32)  128 us
    psum x1, waiting for transfers between devices, on_device(): lax.psum(right_part.astype(jnp.bfloat16), 'col').astype(jnp.float32)  60.9 us
    all_to_all x3, waiting for transfers between devices, copy_for_each(): return lax.all_to_all(copies, axis, split_axis=0, concat_axis=0, tiled=True)  20.5 us
    all_to_all x1, blocking collectives, copy_for_each(): return lax.all_to_all(copies, axis, split_axis=0, concat_axis=0, tiled=True)  19.8 us
    all_to_all x3, starting transfers between devices, copy_for_each(): return lax.all_to_all(copies, axis, split_axis=0, concat_axis=0, tiled=True)  15 us
    dot_general x1, matrix products, on_device(): jnp.einsum('prf,pdf->prd', out_float, d_direction, precision=lax.Precisio...  14.3 us
    dot_general x1, matrix products, on_device(): jnp.einsum('prd,pdf->prf', in_float, d_direction, precision=lax.Precision...  13.3 us
    squeeze x1, local copies, waits for them, and re-layouts, on_device(): gate, up_proj = (summed[0], summed[1])  12.3 us
  transfers between devices with their start and end apart: 6, of which 5 were waited for; matrix products, arithmetic and copies ran while one was open for 13% of the time, Pallas kernels for 0%

commit v1 on v0

--- a/solution.py
+++ b/solution.py
@@ -1,9 +1,18 @@
+import functools
 import jax
 import jax.numpy as jnp
 from jax import lax
 from jax.sharding import PartitionSpec as P
+from jax.lax import all_gather
 
 EPSILON = 1e-06
+
+
+def _measure_cubes(piece_in, axis_id):
+    return all_gather(piece_in, axis_name=axis_id).sum(axis=0)
+
+
+frames_launch = functools.partial(_measure_cubes, axis_id="col")
 
 
 def copy_for_each(value, axis):
@@ -53,7 +62,7 @@
     token_all = gathered_copies(tokens, "row", 0)
     share_rows = token_all.shape[0] // lax.axis_size("col")
     partial_value = jnp.einsum("td,pdf->ptf", token_all, merged, preferred_element_type=jnp.float32)
-    summed = lax.psum(partial_value.astype(jnp.bfloat16), "col").astype(jnp.float32)
+    summed = frames_launch(partial_value.astype(jnp.bfloat16)).astype(jnp.float32)
     gate, up_proj = (summed[0], summed[1])
     hidden_all = (gate * jax.nn.sigmoid(gate) * up_proj).astype(jnp.bfloat16)
     hidden = lax.dynamic_slice_in_dim(hidden_all, lax.axis_index("col") * share_rows, share_rows, 0)

time: 372 us -> 906 us (2.44)
  waiting for transfers between devices: 211 us -> 705 us
  other arithmetic: 30.1 us -> 68 us
    all_gather x0 -> x1, waiting for transfers between devices: none -> 620 us  [_measure_cubes(): return all_gather(piece_in, axis_name=axis_id).sum(axis=0)]
    psum x1 -> x0, waiting for transfers between devices: 128 us -> none  [on_device(): lax.psum(partial_value.astype(jnp.bfloat16), 'col').astype(jnp.float32)]
    reduce_sum x0 -> x1, other arithmetic: none -> 41.3 us  [_measure_cubes(): return all_gather(piece_in, axis_name=axis_id).sum(axis=0)]
    convert_element_type x0 -> x1, local copies, waits for them, and re-layouts: none -> 9.98 us  [on_device(): partial_value.astype(jnp.bfloat16)]
  transfers between devices with their start and end apart: 6 -> 6, of which waited for: 5 -> 4; matrix products, arithmetic and copies ran while one was open for 13% -> 8% of each run, Pallas kernels for 0% -> 0%
where the time goes in v1:
time: 906 us; the launch traced here: 905 us
  waiting for transfers between devices  705 us (78%)
  other arithmetic  68 us (8%)
  matrix products  58.8 us (6%)
  local copies, waits for them, and re-layouts  25.6 us (3%)
  blocking collectives  17.7 us (2%)
  starting transfers between devices  15.5 us (2%)
  between operations  13.8 us (2%)
    all_gather x1, waiting for transfers between devices, _measure_cubes(): return all_gather(piece_in, axis_name=axis_id).sum(axis=0)  620 us
    psum x1, waiting for transfers between devices, on_device(): lax.psum(right_part.astype(jnp.bfloat16), 'col').astype(jnp.float32)  64.8 us
    reduce_sum x1, other arithmetic, _measure_cubes(): return all_gather(piece_in, axis_name=axis_id).sum(axis=0)  41.3 us
    all_to_all x3, waiting for transfers between devices, copy_for_each(): return lax.all_to_all(copies, axis, split_axis=0, concat_axis=0, tiled=True)  20.4 us
  transfers between devices with their start and end apart: 6, of which 4 were waited for; matrix products, arithmetic and copies ran while one was open for 8% of the time, Pallas kernels for 0%

profile of v1, /device:TPU:0, one launch (start us, length us, event | category | flops | bytes accessed | tf_op | source)
XLA Modules:
  0.0 904.9 jit_solution(647256329067684743)
XLA Ops:
  7.2 1.2 copy-done
  8.4 8.6 multiply_reduce_fusion
  17.1 17.7 %all_to_all.20 = f32[16,2,3584]{2,1,0:T(2,128)S(1)} all-to-all(f32[16,2,3584]{2,1,0:T(2,128)S(1)} %broadcast_in_dim.15), channel_id=1, replica_groups=mesh['row'=8,'col'=16] {'col'}, dimensions={0} | all-to-all | bytes 917504 | tf_op jit(solution)/shard_map/all_to_all | solution.py:20
  35.7 5.3 all-to-all-start.1
  41.2 10.1 %all-to-all-done.1 = bf16[8,64,512]{2,1,0:T(8,128)(2,1)S(1)} async-done(((bf16[8,64,512]{2,1,0:T(8,128)(2,1)}), bf16[8,64,512]{2,1,0:T(8,128)(2,1)S(1)}, u32[]{:S(2)}, u32[]{:S(2)}) %all-to-all-start.1) | async-done | bytes 524320 | tf_op jit(solution)/shard_map/all_to_all | solution.py:20
  51.3 11.3 %fusion.12 = bf16[2,512,3584]{1,2,0:T(8,128)(2,1)} fusion(bf16[512,512,1]{1,0,2:T(8,128)(2,1)S(1)} %bitcast.52, f32[2,512,3584]{2,1,0:T(8,128)} %get-tuple-element.12, f32[2,3584]{1,0:T(2,128)S(1)} %fusion.30), kind=kOutput, calls=%fused_computation.23 | convolution fusion | flops 3769106432 | bytes 22573056 | tf_op jit(solution)/shard_map/td,pdf->ptf/dot_general | solution.py:64
  62.7 10.0 %copy.24 = bf16[2,512,3584]{2,1,0:T(8,128)(2,1)} copy(bf16[2,512,3584]{1,2,0:T(8,128)(2,1)} %fusion.12) | data formatting | bytes 14680064 | tf_op jit(solution)/shard_map/convert_element_type | solution.py:65
  73.4 619.7 %all-gather.6.cloned.1.call-done = bf16[32,512,3584]{2,1,0:T(8,128)(2,1)} async-done(((bf16[2,512,3584]{2,1,0:T(8,128)(2,1)}), bf16[32,512,3584]{2,1,0:T(8,128)(2,1)}) %all-gather.6.cloned.1.call-update) | async-done | bytes 117440528 | tf_op jit(solution)/shard_map/all_gather | solution.py:12
  693.1 41.3 %reduce_sum.59 = bf16[2,512,3584]{2,1,0:T(8,128)(2,1)} reduce(bf16[16,2,512,3584]{3,2,1,0:T(8,128)(2,1)} %bitcast.3, bf16[]{:T(256)} %constant.4.clone.1), dimensions={0}, to_apply=%region_2.0 | reduce | flops 55050240 | bytes 124780544 | tf_op jit(solution)/shard_map/reduce_sum | solution.py:12
  734.4 10.4 %convert_element_type.53 = f32[2,512,3584]{2,1,0:T(8,128)} convert(bf16[2,512,3584]{2,1,0:T(8,128)(2,1)} %reduce_sum.59) | non-fusion elementwise | flops 3670016 | bytes 22020096 | tf_op jit(solution)/shard_map/convert_element_type | solution.py:65
  744.8 9.8 %fusion.20 = (bf16[1,512,3584]{2,1,0:T(8,128)(2,1)S(1)}, bf16[1,512,3584]{2,1,0:T(8,128)(2,1)S(1)}, f32[512,3584]{1,0:T(8,128)}) fusion(bf16[512,3584]{1,0:T(8,128)(2,1)} %all-gather.4.cloned.1.call-done, f32[2,512,3584]{2,1,0:T(8,128)} %convert_element_type.53), kind=kLoop, calls=%fused_computation.28 | loop fusion | flops 25690112 | bytes 33030144 | tf_op jit(solution)/shard_map/stack | solution.py:71
  754.6 10.6 %fusion.1 = (f32[2,3584]{1,0:T(2,128)S(1)}, f32[2,3584,512]{1,2,0:T(8,128)}) fusion(f32[2,512,3584]{2,1,0:T(8,128)} %get-tuple-element.12, bf16[512,512,1]{1,0,2:T(8,128)(2,1)S(1)} %bitcast.53, bf16[1,512,3584]{2,1,0:T(8,128)(2,1)S(1)} %get-tuple-element.5, bf16[1,512,3584]{2,1,0:T(8,128)(2,1)S(1)} %get-tuple-element.4), kind=kOutput, calls=%fused_computation.3 | convolution fusion | flops 3769099264 | bytes 37253120 | tf_op jit(solution)/shard_map/td,ptf->pdf/dot_general | solution.py:72
  765.2 0.9 broadcast_in_dim.17
  766.0 5.2 all-to-all-start.2
  771.6 10.3 %all-to-all-done.2 = f32[16,2,3584]{2,1,0:T(2,128)S(1)} async-done(((f32[16,2,3584]{2,1,0:T(2,128)}), f32[16,2,3584]{2,1,0:T(2,128)S(1)}, u32[]{:S(2)}, u32[]{:S(2)}) %all-to-all-start.2) | async-done | bytes 458784 | tf_op jit(solution)/shard_map/all_to_all | solution.py:20
  782.7 14.1 %fusion.16 = bf16[2,64,3584]{2,1,0:T(8,128)(2,1)} fusion(bf16[2,64,512]{2,1,0:T(8,128)(2,1)S(1)} %copy-done.1, f32[2,3584,512]{1,2,0:T(8,128)} %get-tuple-element.14, f32[2,512,3584]{2,1,0:T(8,128)} %get-tuple-element.12, f32[2,3584]{1,0:T(2,128)S(1)} %get-tuple-element.10, f32[2,3584]{1,0:T(2,128)S(1)} %fusion.30), kind=kOutput, calls=%fused_computation.26 | convolution fusion | flops 2830041088 | bytes 30466048 | tf_op jit(solution)/shard_map/prd,pdf->prf/dot_general | solution.py:77
  796.8 14.2 %fusion.24 = bf16[2,64,512]{2,1,0:T(8,128)(2,1)S(1)} fusion(bf16[2,64,3584]{2,1,0:T(8,128)(2,1)S(1)} %copy-done, f32[2,3584,512]{1,2,0:T(8,128)} %get-tuple-element.14, f32[2,512,3584]{2,1,0:T(8,128)} %get-tuple-element.12, f32[2,3584]{1,0:T(2,128)S(1)} %get-tuple-element.10, f32[2,3584]{1,0:T(2,128)S(1)} %fusion.30), kind=kOutput, calls=%fused_computation.31 | convolution fusion | flops 2829647872 | bytes 30466048 | tf_op jit(solution)/shard_map/prf,pdf->prd/dot_general | solution.py:79
  811.0 1.1 broadcast_in_dim.18
  812.2 4.4 all-to-all-start.3
  816.6 11.5 %slice_bitcast_fusion.1 = (f32[512,3584]{1,0:T(8,128)}, f32[512,3584]{1,0:T(8,128)}) fusion(f32[2,512,3584]{2,1,0:T(8,128)} %convert_element_type.53), kind=kLoop, calls=%fused_computation.16 | loop fusion | bytes 29360128 | tf_op jit(solution)/shard_map/squeeze | solution.py:66
  828.0 2.1 fusion.27
  830.1 64.8 %all-reduce.2.cloned.1.call-done = bf16[2,64,3584]{2,1,0:T(8,128)(2,1)} async-done(((bf16[2,64,3584]{2,1,0:T(8,128)(2,1)}), bf16[2,64,3584]{2,1,0:T(8,128)(2,1)}) %all-reduce.2.cloned.1.call-update) | async-done | bytes 917520 | tf_op jit(solution)/shard_map/psum | solution.py:78
  894.9 2.6 convert_element_type.63
  897.5 0.8 convert_reduce_fusion
  (21 shorter events, 3.1 us)
Async XLA Ops:
  7.2 1.2 copy-start
  8.4 26.5 %copy-start.3 = (bf16[64,512]{1,0:T(8,128)(2,1)S(1)}, bf16[64,512]{1,0:T(8,128)(2,1)}, u32[]{:S(2)}) copy-start(bf16[64,512]{1,0:T(8,128)(2,1)} %param.6) | copy-start | bytes 196612
  8.4 32.8 %copy-start.2 = (f32[2,3584]{1,0:T(2,128)S(1)}, f32[2,3584]{1,0:T(2,128)}, u32[]{:S(2)}) copy-start(f32[2,3584]{1,0:T(2,128)} %param.10) | copy-start | bytes 86020
  35.7 15.6 %all-to-all-start.1 = ((bf16[8,64,512]{2,1,0:T(8,128)(2,1)}), bf16[8,64,512]{2,1,0:T(8,128)(2,1)S(1)}, u32[]{:S(2)}, u32[]{:S(2)}) async-start(bf16[8,64,512]{2,1,0:T(8,128)(2,1)} %broadcast_in_dim.16), calls=%async_computation.1 | async-start | bytes 1048576 | tf_op jit(solution)/shard_map/all_to_all | solution.py:20
  41.0 652.1 %all-gather.6.cloned.1.call-start = ((), (), s32[]{:S(2)}) async-start(), calls=%async_computation.6 | async-start | bytes 124780544 | tf_op jit(solution)/shard_map/all_gather | solution.py:12
  72.7 672.1 %all-gather.4.cloned.1.call-start = ((), (), s32[]{:S(2)}) async-start(), calls=%async_computation.4 | async-start | bytes 3899392 | tf_op jit(solution)/shard_map/all_gather | solution.py:69
  754.6 28.2 %copy-start.1 = (bf16[2,64,512]{2,1,0:T(8,128)(2,1)S(1)}, bf16[2,64,512]{2,1,0:T(8,128)(2,1)}, u32[]{:S(2)}) copy-start(bf16[2,64,512]{2,1,0:T(8,128)(2,1)} %param.8) | copy-start | bytes 393220
  766.0 15.9 %all-to-all-start.2 = ((f32[16,2,3584]{2,1,0:T(2,128)}), f32[16,2,3584]{2,1,0:T(2,128)S(1)}, u32[]{:S(2)}, u32[]{:S(2)}) async-start(f32[16,2,3584]{2,1,0:T(2,128)} %broadcast_in_dim.17), calls=%async_computation.2 | async-start | bytes 917504 | tf_op jit(solution)/shard_map/all_to_all | solution.py:20
  771.3 123.6 %all-reduce.2.cloned.1.call-start = ((), (), s32[]{:S(2)}) async-start(), calls=%async_computation.5 | async-start | bytes 1835008 | tf_op jit(solution)/shard_map/psum | solution.py:78
  812.2 85.4 %all-to-all-start.3 = ((bf16[8,2,64,512]{3,2,1,0:T(8,128)(2,1)}), bf16[8,2,64,512]{3,2,1,0:T(8,128)(2,1)S(1)}, u32[]{:S(2)}, u32[]{:S(2)}) async-start(bf16[8,2,64,512]{3,2,1,0:T(8,128)(2,1)} %broadcast_in_dim.18), calls=%async_computation.3 | async-start | bytes 2097152 | tf_op jit(solution)/shard_map/all_to_all | solution.py:20
Sparse Core Ops, SparseCore 0:
  72.8 620.2 all-gather.5
  695.2 49.0 all-gather.3
  811.2 83.7 all-reduce.1
